TPU v7x, 256 devices: a whole 4x4x8 slice. The times are simulated.
256 devices in a mesh: dp: 4 (over x), ctx: 64 (over z, y, core).
Axes of the slice: x: 4, y: 4, z: 8, core: 2. Of those that a mesh axis runs over, the one named last changes fastest.
Arguments:
- queries: bfloat16 [2, 32768, 2048], P(None, ('dp', 'ctx')), may hold values from -6 to 6
- keys: bfloat16 [2, 32768, 1024], P(None, ('dp', 'ctx')), may hold values from -6 to 6
- values: bfloat16 [2, 32768, 1024], P(None, ('dp', 'ctx')), may hold values from -6 to 6
- doc_start: int32 [2, 32768], P(None, ('dp', 'ctx')), may hold values from 0 to 16383, as said below
- gain_q: float32 [128], replicated, may hold values from 0.5 to 1.5
- key_norm_gain: float32 [128], replicated, may hold values from 0.5 to 1.5
- cotangent: bfloat16 [2, 32768, 2048], P(None, ('dp', 'ctx')), may hold values from -6 to 6
Outputs:
- attended: bfloat16 [2, 32768, 2048], P(None, ('dp', 'ctx'))
- grad_queries: bfloat16 [2, 32768, 2048], P(None, ('dp', 'ctx'))
- grad_keys: bfloat16 [2, 32768, 1024], P(None, ('dp', 'ctx'))
- value_gradients: bfloat16 [2, 32768, 1024], P(None, ('dp', 'ctx'))
- grad_gain_q: float32 [128], replicated
- grad_gain_k: float32 [128], replicated
Inputs may be any that keep to these rules, and one draw needn't show every extreme that they name: doc_start gives each token the position in its sequence of its document's first token; the documents of a sequence are runs of 1 to 256 tokens, the first starting at 0, and every sequence has one of exactly 256 tokens.
All inputs are finite; a program needn't handle non-finite values.
Results may differ from a plain program's by a relative error of at most 0.012.
Values may be sent and summed in bfloat16 or wider, within the bound.
No kernel may reach another device: no remote copies, remote signals or barrier semaphores. Data moves between devices by JAX's collectives and lax.ppermute only.
A program may use at most 128 MiB of HBM per device.

v0:
```python
from functools import partial
import jax
import jax.numpy as jnp
from jax import lax
from jax.sharding import PartitionSpec as P

REACH = 2
query_factor = 168.0 ** (-0.5)
rotary_base = 1000000.0
norm_epsilon = 1e-06


def from_behind(block, axis, distance):
    devices = range(lax.axis_size(axis))
    route = [(i - distance, i) for i in devices if i - distance in devices]
    return lax.ppermute(block, axis, route)


def rotary_angles(position, head_width):
    exponent = jnp.arange(head_width // 2, dtype=jnp.float32) * (2.0 / head_width)
    frequency = jnp.exp(-exponent * jnp.log(jnp.float32(rotary_base)))
    return position.astype(jnp.float32)[..., None] * frequency


def prepare(tensor, gain, angle, factor):
    inverse = lax.rsqrt(jnp.mean(tensor * tensor, axis=-1, keepdims=True) + norm_epsilon)
    normed = tensor * inverse * gain
    middle = tensor.shape[-1] // 2
    cosine = jnp.cos(angle)[..., None, :]
    sine = jnp.sin(angle)[..., None, :]
    first = normed[..., :middle]
    second = normed[..., middle:]
    return (
        jnp.concatenate([first * cosine - second * sine, second * cosine + first * sine], axis=-1)
        * factor
    )


def slot_positions(slot, rows, group, block):
    ascending = slot * block + rows
    descending = slot * block + block - 1 - rows
    inside = (slot >= 0) & (slot < 2 * group)
    return jnp.where(inside, jnp.where(slot < group, ascending, descending), -1)


def visible(doc_query, query_position, key_position):
    return (doc_query[:, :, None] <= key_position[:, None, :]) & (
        key_position[:, None, :] <= query_position[:, :, None]
    )


def forward_terms(q_rot, key_panel, value_panel, mask):
    scores = jnp.einsum("xihrd,xjhd->xhrij", q_rot, key_panel, preferred_element_type=jnp.float32)
    weights = jnp.where(mask[:, None, None], jnp.exp(scores), 0.0)
    summed = jnp.sum(weights, axis=-1)
    mixed = jnp.einsum(
        "xhrij,xjhd->xihrd",
        weights.astype(jnp.bfloat16),
        value_panel,
        preferred_element_type=jnp.float32,
    )
    return (summed, mixed)


def softmax_grads(q_rot, cotangent_heads, key_panel, value_panel, mask, total, delta):
    scores = jnp.einsum("xihrd,xjhd->xhrij", q_rot, key_panel, preferred_element_type=jnp.float32)
    probs = jnp.where(mask[:, None, None], jnp.exp(scores) / total[..., None], 0.0)
    dprob = jnp.einsum(
        "xihrd,xjhd->xhrij", cotangent_heads, value_panel, preferred_element_type=jnp.float32
    )
    dscore = probs * (dprob - delta[..., None])
    return (probs.astype(jnp.bfloat16), dscore.astype(jnp.bfloat16))


def key_grads(probs, dscore, q_rot, cotangent_heads):
    grad_key = jnp.einsum("xhrij,xihrd->xjhd", dscore, q_rot, preferred_element_type=jnp.float32)
    grad_value = jnp.einsum(
        "xhrij,xihrd->xjhd", probs, cotangent_heads, preferred_element_type=jnp.float32
    )
    return (grad_key, grad_value)


def all_grads(q_rot, cotangent_heads, key_panel, value_panel, mask, total, delta):
    probs, dscore = softmax_grads(
        q_rot, cotangent_heads, key_panel, value_panel, mask, total, delta
    )
    grad_key, grad_value = key_grads(probs, dscore, q_rot, cotangent_heads)
    grad_query = jnp.einsum(
        "xhrij,xjhd->xihrd", dscore, key_panel, preferred_element_type=jnp.float32
    )
    return (grad_query, grad_key, grad_value)


def advance(lower, upper, at_fold):
    moved_lower = from_behind(lower, "ctx", 1)
    moved_upper = from_behind(upper, "ctx", -1)
    return (moved_lower, jnp.where(at_fold, lower, moved_upper))


def retreat_grads(lower, upper, at_fold, at_start):
    moved_lower = from_behind(lower, "ctx", -1)
    moved_upper = from_behind(upper, "ctx", 1)
    return (jnp.where(at_fold, upper, moved_lower), jnp.where(at_start, 0.0, moved_upper))


def shards(queries, keys, values, doc_start, gain_q, key_norm_gain, cotangent):
    group = lax.axis_size("ctx")
    block = queries.shape[1]
    head_width = gain_q.shape[0]
    q_heads = queries.shape[2] // head_width
    kv_heads = keys.shape[2] // head_width
    repeat = q_heads // kv_heads
    group_index = lax.axis_index("ctx")
    at_fold = group_index == group - 1
    at_start = group_index == 0
    rows = jnp.arange(block, dtype=jnp.int32)[None, :]
    own_slot = jnp.stack([group_index, 2 * group - 1 - group_index])[:, None]
    own_position = slot_positions(own_slot, rows, group, block)
    angle = rotary_angles(own_position, head_width)
    q_rotated, q_back = jax.vjp(
        lambda tensor, gain: prepare(tensor, gain, angle, query_factor),
        queries.astype(jnp.float32).reshape(2, block, q_heads, head_width),
        gain_q,
    )
    q_rot = q_rotated.astype(jnp.bfloat16).reshape(2, block, kv_heads, repeat, head_width)
    k_rotated, k_back = jax.vjp(
        lambda tensor, gain: prepare(tensor, gain, angle, 1.0),
        keys.astype(jnp.float32).reshape(2, block, kv_heads, head_width),
        key_norm_gain,
    )
    k_rot = k_rotated.astype(jnp.bfloat16)
    cotangent_heads = cotangent.reshape(2, block, kv_heads, repeat, head_width)
    local_key_panel = jnp.stack([k_rot.reshape(2, block, -1), values], axis=1)
    panels = [local_key_panel]
    lower, upper = (local_key_panel[0], local_key_panel[1])
    for step in range(REACH):
        lower, upper = advance(lower, upper, at_fold)
        panels.append(jnp.stack([lower, upper]))
    masks = [
        visible(doc_start, own_position, slot_positions(own_slot - step, rows, group, block))
        for step in range(REACH + 1)
    ]
    zeros_q = jnp.zeros((2, block, kv_heads, repeat, head_width), jnp.float32)
    summed = jnp.zeros((2, kv_heads, repeat, block), jnp.float32)
    mixed = zeros_q
    key_panels = []
    value_panels = []
    for step in range(REACH + 1):
        key_panel = panels[step][:, 0].reshape(2, block, kv_heads, head_width)
        value_panel = panels[step][:, 1].reshape(2, block, kv_heads, head_width)
        key_panels.append(key_panel)
        value_panels.append(value_panel)
        compute = partial(forward_terms, q_rot, key_panel, value_panel, masks[step])
        if step == 0:
            terms = compute()
        else:
            terms = compute()
        summed = summed + terms[0]
        mixed = mixed + terms[1]
    attended_heads = (mixed / jnp.transpose(summed, (0, 3, 1, 2))[..., None]).astype(jnp.bfloat16)
    delta = jnp.einsum(
        "xihrd,xihrd->xhri", cotangent_heads, attended_heads, preferred_element_type=jnp.float32
    )
    grad_q_heads = zeros_q
    for step in range(REACH, -1, -1):
        compute = partial(
            all_grads,
            q_rot,
            cotangent_heads,
            key_panels[step],
            value_panels[step],
            masks[step],
            summed,
            delta,
        )
        if step == 0:
            terms = compute()
        else:
            terms = compute()
        grad_q_heads = grad_q_heads + terms[0]
        contribution = jnp.stack(
            [terms[1].reshape(2, block, -1), terms[2].reshape(2, block, -1)], axis=1
        )
        if step == REACH:
            carried_lower, carried_upper = (contribution[0], contribution[1])
        else:
            carried_lower, carried_upper = retreat_grads(
                carried_lower, carried_upper, at_fold, at_start
            )
            carried_lower = carried_lower + contribution[0]
            carried_upper = carried_upper + contribution[1]
    key_value_gradient = jnp.stack([carried_lower, carried_upper])
    grad_k_heads = key_value_gradient[:, 0].reshape(2, block, kv_heads, head_width)
    grad_v_flat = key_value_gradient[:, 1]
    grad_queries, grad_gain_q = q_back(grad_q_heads.reshape(2, block, q_heads, head_width))
    grad_keys, grad_gain_k = k_back(grad_k_heads)
    grad_gain_q, grad_gain_k = lax.psum((grad_gain_q, grad_gain_k), ("dp", "ctx"))
    return (
        attended_heads.reshape(2, block, -1),
        grad_queries.reshape(2, block, -1).astype(jnp.bfloat16),
        grad_keys.reshape(2, block, -1).astype(jnp.bfloat16),
        grad_v_flat.astype(jnp.bfloat16),
        grad_gain_q,
        grad_gain_k,
    )


def solution(mesh):
    placed = (
        P(None, ("dp", "ctx"), None),
        P(None, ("dp", "ctx"), None),
        P(None, ("dp", "ctx"), None),
        P(None, ("dp", "ctx")),
        P(),
        P(),
        P(None, ("dp", "ctx"), None),
    )
    return jax.shard_map(
        shards,
        mesh=mesh,
        in_specs=placed,
        out_specs=(
            P(None, ("dp", "ctx"), None),
            P(None, ("dp", "ctx"), None),
            P(None, ("dp", "ctx"), None),
            P(None, ("dp", "ctx"), None),
            P(),
            P(),
        ),
        check_vma=False,
    )
```

profile of v0, /device:TPU:1, one launch (start us, length us, event | category | flops | bytes accessed | tf_op | source)
XLA Modules:
  0.0 234.9 jit_solution(2773730723189249938)
XLA Ops:
  8.4 5.1 %collective-permute-start.1 = (bf16[2,128,1024]{1,2,0:T(8,128)(2,1)}, bf16[2,128,1024]{1,2,0:T(8,128)(2,1)}, u32[]{:S(2)}, u32[]{:S(2)}) collective-permute-start(bf16[2,128,1024]{1,2,0:T(8,128)(2,1)} %fusion.65), channel_id=1, source_target_pairs={{1,0},{2,1},{3,2},{4,3},{5,4},{6,5},{7,6},{8,7},{9,8},{10,9},{11,1... | collective-permute-start | bytes 1572872 | tf_op jit(solution)/shard_map/ppermute | solution.py:16
  17.4 2.0 copy.219
  19.3 1.9 copy.220
  21.5 2.9 %fusion.3 = bf16[2,128,8,2,128]{4,1,3,2,0:T(8,128)(2,1)S(1)} fusion(f32[2,128,8,2,64]{4,1,3,2,0:T(8,128)} %bitcast.308, f32[2,128,8,2,64]{4,1,3,2,0:T(8,128)} %bitcast.307), kind=kLoop, calls=%fused_computation.9 | loop fusion | flops 1572864 | bytes 3145728 | tf_op jit(solution)/shard_map/convert_element_type | solution.py:125
  25.4 2.1 broadcast_select_fusion
  27.5 1.9 collective-permute-start
  29.4 2.4 %fusion.15 = (f32[2,8,2,128]{3,2,1,0:T(2,128)}, f32[2,8,128,128,2]{3,2,4,1,0:T(8,128)}) fusion(pred[2,128,128]{1,2,0:T(8,128)(4,1)S(1)} %get-tuple-element.68, bf16[2,128,8,2,128]{4,1,3,2,0:T(8,128)(2,1)S(1)} %fusion.3, bf16[2,128,8,128]{3,1,2,0:T(8,128)(2,1)S(1)} %copy-done.9), kind=kOutput, calls=%fused_computation.48 | convolution fusion | flops 135262208 | bytes 3719168 | tf_op jit(solution)/shard_map/xihrd,xjhd->xhrij/dot_general | solution.py:53
  31.8 3.2 %collective-permute-start.3 = (bf16[2,128,1024]{1,2,0:T(8,128)(2,1)}, bf16[2,128,1024]{1,2,0:T(8,128)(2,1)}, u32[]{:S(2)}, u32[]{:S(2)}) collective-permute-start(bf16[2,128,1024]{1,2,0:T(8,128)(2,1)} %get-tuple-element.48), channel_id=1, source_target_pairs={{1,0},{2,1},{3,2},{4,3},{5,4},{6,5},{7,6},{8,7},{9,8},{10,9},{11,1... | collective-permute-start | bytes 1572872 | tf_op jit(solution)/shard_map/ppermute | solution.py:16
  35.9 2.6 %reshape.655 = bf16[2,128,8,2,128]{4,3,2,1,0:T(2,128)(2,1)} reshape(bf16[2,128,2048]{2,1,0:T(8,128)(2,1)} %param.13) | data formatting | bytes 2097152 | tf_op jit(solution)/shard_map/reshape | solution.py:132
  38.4 3.7 %copy.247 = bf16[2,128,8,2,128]{1,4,3,2,0:T(8,128)(2,1)} copy(bf16[2,128,8,2,128]{4,3,2,1,0:T(2,128)(2,1)} %reshape.655) | data formatting | bytes 2097152 | tf_op jit(solution)/shard_map/reshape | solution.py:132
  42.1 2.7 %collective-permute-start.2 = (bf16[2,128,1024]{1,2,0:T(8,128)(2,1)}, bf16[2,128,1024]{1,2,0:T(8,128)(2,1)S(1)}, u32[]{:S(2)}, u32[]{:S(2)}) collective-permute-start(bf16[2,128,1024]{1,2,0:T(8,128)(2,1)} %collective-permute-done), channel_id=1, source_target_pairs={{0,1},{1,2},{2,3},{3,4},{4,5},{5,6},{6,7},{7,8},{8,9},{9,10},{10,1... | collective-permute-start | bytes 1572872 | tf_op jit(solution)/shard_map/ppermute | solution.py:16
  48.7 2.3 collective-permute-done.2
  54.2 2.4 %bitcast_convert_fusion = (f32[2,8,2,128,128]{3,4,2,1,0:T(8,128)}, bf16[2,128,8,2,128]{1,4,3,2,0:T(8,128)(2,1)}) fusion(f32[2,128,8,2]{1,3,2,0:T(2,128)S(1)} %bitcast.339, f32[2,8,128,2,128]{4,2,3,1,0:T(8,128)S(1)} %fusion.23, f32[2,8,128,2,128]{4,2,3,1,0:T(8,128)S(1)} %fusion.25, f32[2,8,128,128,2]{3,2,4,1,0:T(8,128)S(1)} %copy-done.29, ...), kind=kOutput, calls=%fused_computation.87 | convolution fusion | flops 137887744 | bytes 10010624 | tf_op jit(solution)/shard_map/xhrij,xjhd->xihrd/dot_general | solution.py:56
  56.6 4.2 %copy.285 = f32[2,8,2,128,128]{4,2,1,3,0:T(2,128)} copy(f32[2,8,2,128,128]{3,4,2,1,0:T(8,128)} %get-tuple-element.90) | data formatting | bytes 4194304
  60.8 5.1 %multiply_reduce_fusion = f32[2,8,2,128]{2,1,3,0:T(8,128)} fusion(f32[2,8,2,128,128]{4,2,1,3,0:T(2,128)} %copy.285, bf16[2,128,8,2,128]{4,3,2,1,0:T(2,128)(2,1)} %reshape.655), kind=kLoop, calls=%fused_computation.40 | loop fusion | flops 1568768 | bytes 3162112
  65.9 2.2 copy.286
  68.1 2.5 %fusion.49 = f32[2,8,128,128,1]{2,3,4,1,0:T(8,128)S(1)} fusion(bf16[2,128,8,2,128]{1,4,3,2,0:T(8,128)(2,1)} %copy.247, f32[2,8,128,128,2]{3,2,4,1,0:T(8,128)} %copy-done.13, f32[2,8,2,128]{3,2,1,0:T(2,128)} %bitcast.340, pred[2,128,128]{1,2,0:T(8,128)(4,1)} %get-tuple-element.69), kind=kOutput, calls=%fused_computation.97 | convolution fusion | flops 135790592 | bytes 4243456 | tf_op jit(solution)/shard_map/xhrij,xihrd->xjhd/dot_general | solution.py:77
  75.7 2.1 collective-permute-start.5
  80.8 11.8 %collective-permute-done.5 = f32[2,128,1024]{1,2,0:T(8,128)S(1)} collective-permute-done((f32[2,128,1024]{1,2,0:T(8,128)S(1)}, f32[2,128,1024]{1,2,0:T(8,128)S(1)}, u32[]{:S(2)}, u32[]{:S(2)}) %collective-permute-start.5) | collective-permute-done | bytes 1048608 | tf_op jit(solution)/shard_map/ppermute | solution.py:16
  94.1 1.9 collective-permute-start.4
  96.0 3.6 %collective-permute-start.6 = (f32[2,128,1024]{1,2,0:T(8,128)}, f32[2,128,1024]{1,2,0:T(8,128)}, u32[]{:S(2)}, u32[]{:S(2)}) collective-permute-start(f32[2,128,1024]{1,2,0:T(8,128)} %get-tuple-element.44), channel_id=1, source_target_pairs={{1,0},{2,1},{3,2},{4,3},{5,4},{6,5},{7,6},{8,7},{9,8},{10,9},{11,1... | collective-permute-start | bytes 3145736 | tf_op jit(solution)/shard_map/ppermute | solution.py:16
  101.1 3.3 %copy.325 = f32[2,128,16,64]{3,2,1,0:T(8,128)} copy(f32[2,128,16,64]{1,3,2,0:T(8,128)} %get-tuple-element.58) | data formatting | bytes 2097152
  104.4 3.3 %copy.326 = f32[2,128,16,64]{3,2,1,0:T(8,128)} copy(f32[2,128,16,64]{1,3,2,0:T(8,128)} %get-tuple-element.59) | data formatting | bytes 2097152
  107.7 1.9 fusion.89
  112.5 3.0 %fusion.32 = (f32[1,2,128,1024]{2,3,1,0:T(8,128)S(1)}, f32[2,128,1024]{1,2,0:T(8,128)}) fusion(f32[2,1,128,1024]{2,3,1,0:T(8,128)S(1)} %bitcast.301, f32[2,1,128,1024]{2,3,1,0:T(8,128)S(1)} %bitcast.319, f32[2,128,1024]{1,2,0:T(8,128)} %collective-permute-done.6, pred[]{:T(512)S(6)} %eq.6, f32[2,1,128,1024]{2,3,1,0:T(8,128)S(1)} %bitcast.323, ...), kind=kLoop, calls=%fused_computation.63 | loop fusion | flops 1572864 | bytes 8388610 | tf_op jit(solution)/shard_map/stack | solution.py:192
  115.5 2.0 collective-permute-start.7
  118.2 2.5 %multiply_reduce_fusion.1 = (f32[128]{0:T(128)}, f32[2,128,16]{2,1,0:T(8,128)}) fusion(f32[2,128,16]{2,1,0:T(8,128)S(1)} %copy.218, f32[2,128,16,64]{3,2,1,0:T(8,128)S(1)} %get-tuple-element.53, f32[2,128,16,64]{3,2,1,0:T(8,128)S(1)} %get-tuple-element.52, f32[128]{0:T(128)S(1)} %copy-done.60, f32[2,128,16,128]{3,2,1,0:T(8,128)S(1)} %bitcast.299), kind=kLoop, calls=%fused_computation.41 | loop fusion | flops 3665792 | bytes 4228096 | tf_op jit(solution)/shard_map/transpose(jvp())/reduce_sum | solution.py:27
  120.7 1.6 copy.242
  125.1 4.8 %fusion = bf16[2,128,16,128]{3,2,1,0:T(8,128)(2,1)} fusion(f32[2,128,16]{2,1,0:T(8,128)} %copy.243, f32[128]{0:T(128)} %param.11, f32[2,128,16]{2,1,0:T(8,128)S(1)} %copy.218, f32[2,128,16,64]{3,2,1,0:T(8,128)} %copy-done.1, f32[2,128,16,64]{3,2,1,0:T(8,128)} %copy-done, f32[2,128,16,128]{3,2,1,0:T(8,128)S(1)} %bitcast.300), kind=kLoop, calls=%fused_computation.1 | loop fusion | flops 3670016 | bytes 5276160 | tf_op jit(solution)/shard_map/convert_element_type | solution.py:200
  129.9 2.4 %convert_element_type.84 = bf16[2,128,2048]{2,1,0:T(8,128)(2,1)} reshape(bf16[2,128,16,128]{3,2,1,0:T(8,128)(2,1)} %fusion) | data formatting | bytes 2097152 | tf_op jit(solution)/shard_map/convert_element_type | solution.py:200
  139.0 1.6 multiply_add_fusion.4
  143.9 91.0 %all-reduce.4 = (f32[128]{0:T(128)}, f32[128]{0:T(128)}) all-reduce(f32[128]{0:T(128)S(1)} %copy-done.72, f32[128]{0:T(128)S(1)} %get-tuple-element.38), channel_id=1, replica_groups=mesh['dp'=4,'ctx'=64] {'dp','ctx'}, use_global_device_ids=true, to_apply=%region_8.9 | all-reduce | flops 256 | bytes 2048 | tf_op jit(solution)/shard_map/psum | solution.py:197
  (216 shorter events, 47.2 us)
Async XLA Ops:
  0.6 4.8 %copy-start.61 = (f32[128]{0:T(128)S(1)}, f32[128]{0:T(128)}, u32[]{:S(2)}) copy-start(f32[128]{0:T(128)} %param.12) | copy-start | bytes 1540
  6.5 7.1 %copy-start.8 = (bf16[2,128,8,128]{3,1,2,0:T(8,128)(2,1)}, bf16[2,128,8,128]{3,1,2,0:T(8,128)(2,1)S(1)}, u32[]{:S(2)}) copy-start(bf16[2,128,8,128]{3,1,2,0:T(8,128)(2,1)S(1)} %maximum_convert_fusion) | copy-start | bytes 1572868
  7.2 6.3 %copy-start.19 = (bf16[2,128,8,128]{1,3,2,0:T(8,128)(2,1)}, bf16[2,128,8,128]{1,3,2,0:T(8,128)(2,1)S(1)}, u32[]{:S(2)}) copy-start(bf16[2,128,8,128]{1,3,2,0:T(8,128)(2,1)S(1)} %copy.223) | copy-start | bytes 1572868
  7.5 6.1 %copy-start.21 = (bf16[2,128,1024]{1,2,0:T(8,128)(2,1)}, bf16[2,128,1024]{1,2,0:T(8,128)(2,1)S(1)}, u32[]{:S(2)}) copy-start(bf16[2,128,1024]{1,2,0:T(8,128)(2,1)S(1)} %copy.224) | copy-start | bytes 1572868
  8.4 17.0 %collective-permute-start.1 = (bf16[2,128,1024]{1,2,0:T(8,128)(2,1)}, bf16[2,128,1024]{1,2,0:T(8,128)(2,1)}, u32[]{:S(2)}, u32[]{:S(2)}) collective-permute-start(bf16[2,128,1024]{1,2,0:T(8,128)(2,1)} %fusion.65), channel_id=1, source_target_pairs={{1,0},{2,1},{3,2},{4,3},{5,4},{6,5},{7,6},{8,7},{9,8},{10,9},{11,1... | collective-permute-start | bytes 1572872 | tf_op jit(solution)/shard_map/ppermute | solution.py:16
  21.4 3.1 %copy-start.63 = (pred[2]{0:T(512)(128)(4,1)S(1)}, pred[2]{0:T(512)(128)(4,1)}, u32[]{:S(2)}) copy-start(pred[2]{0:T(512)(128)(4,1)} %get-tuple-element.78) | copy-start | bytes 10
  21.4 3.1 %copy-start.64 = (pred[2]{0:T(512)(128)(4,1)S(1)}, pred[2]{0:T(512)(128)(4,1)}, u32[]{:S(2)}) copy-start(pred[2]{0:T(512)(128)(4,1)} %get-tuple-element.79) | copy-start | bytes 10
  21.4 3.1 %copy-start.65 = (pred[2]{0:T(512)(128)(4,1)S(1)}, pred[2]{0:T(512)(128)(4,1)}, u32[]{:S(2)}) copy-start(pred[2]{0:T(512)(128)(4,1)} %get-tuple-element.80) | copy-start | bytes 10
  21.4 3.1 %copy-start.66 = (pred[2]{0:T(512)(128)(4,1)S(1)}, pred[2]{0:T(512)(128)(4,1)}, u32[]{:S(2)}) copy-start(pred[2]{0:T(512)(128)(4,1)} %get-tuple-element.81) | copy-start | bytes 10
  21.4 3.1 %copy-start.67 = (s32[2]{0:T(128)S(1)}, s32[2]{0:T(128)}, u32[]{:S(2)}) copy-start(s32[2]{0:T(128)} %get-tuple-element.46) | copy-start | bytes 28
  21.5 3.1 %copy-start.58 = (s32[2,128]{1,0:T(2,128)S(1)}, s32[2,128]{1,0:T(2,128)}, u32[]{:S(2)}) copy-start(s32[2,128]{1,0:T(2,128)} %get-tuple-element.51) | copy-start | bytes 3076
  21.5 3.1 %copy-start.71 = (s32[2,128]{1,0:T(2,128)S(1)}, s32[2,128]{1,0:T(2,128)}, u32[]{:S(2)}) copy-start(s32[2,128]{1,0:T(2,128)} %param.10) | copy-start | bytes 3076
  21.5 3.9 %copy-start.20 = (bf16[2,128,8,128]{1,3,2,0:T(8,128)(2,1)S(1)}, bf16[2,128,8,128]{1,3,2,0:T(8,128)(2,1)}, u32[]{:S(2)}) copy-start(bf16[2,128,8,128]{1,3,2,0:T(8,128)(2,1)} %copy-done.19) | copy-start | bytes 1572868
  21.5 3.9 %copy-start.22 = (bf16[2,128,1024]{1,2,0:T(8,128)(2,1)S(1)}, bf16[2,128,1024]{1,2,0:T(8,128)(2,1)}, u32[]{:S(2)}) copy-start(bf16[2,128,1024]{1,2,0:T(8,128)(2,1)} %copy-done.21) | copy-start | bytes 1572868
  24.4 5.0 %copy-start.9 = (bf16[2,128,8,128]{3,1,2,0:T(8,128)(2,1)S(1)}, bf16[2,128,8,128]{3,1,2,0:T(8,128)(2,1)}, u32[]{:S(2)}) copy-start(bf16[2,128,8,128]{3,1,2,0:T(8,128)(2,1)} %copy-done.8) | copy-start | bytes 1572868
  25.4 6.4 %copy-start.49 = (pred[2,128,128]{1,2,0:T(8,128)(4,1)}, pred[2,128,128]{1,2,0:T(8,128)(4,1)S(1)}, u32[]{:S(2)}) copy-start(pred[2,128,128]{1,2,0:T(8,128)(4,1)S(1)} %get-tuple-element.68) | copy-start | bytes 98308
  27.5 14.6 %collective-permute-start = (bf16[2,128,1024]{1,2,0:T(8,128)(2,1)}, bf16[2,128,1024]{1,2,0:T(8,128)(2,1)}, u32[]{:S(2)}, u32[]{:S(2)}) collective-permute-start(bf16[2,128,1024]{1,2,0:T(8,128)(2,1)} %get-tuple-element.49), channel_id=1, source_target_pairs={{0,1},{1,2},{2,3},{3,4},{4,5},{5,6},{6,7},{7,8},{8,9},{9,10},{10,1... | collective-permute-start | bytes 1572872 | tf_op jit(solution)/shard_map/ppermute | solution.py:16
  31.8 14.9 %collective-permute-start.3 = (bf16[2,128,1024]{1,2,0:T(8,128)(2,1)}, bf16[2,128,1024]{1,2,0:T(8,128)(2,1)}, u32[]{:S(2)}, u32[]{:S(2)}) collective-permute-start(bf16[2,128,1024]{1,2,0:T(8,128)(2,1)} %get-tuple-element.48), channel_id=1, source_target_pairs={{1,0},{2,1},{3,2},{4,3},{5,4},{6,5},{7,6},{8,7},{9,8},{10,9},{11,1... | collective-permute-start | bytes 1572872 | tf_op jit(solution)/shard_map/ppermute | solution.py:16
  42.1 4.0 %copy-start.43 = (pred[2,128,128]{1,2,0:T(8,128)(4,1)S(1)}, pred[2,128,128]{1,2,0:T(8,128)(4,1)}, u32[]{:S(2)}) copy-start(pred[2,128,128]{1,2,0:T(8,128)(4,1)} %get-tuple-element.70) | copy-start | bytes 98308
  42.1 8.9 %collective-permute-start.2 = (bf16[2,128,1024]{1,2,0:T(8,128)(2,1)}, bf16[2,128,1024]{1,2,0:T(8,128)(2,1)S(1)}, u32[]{:S(2)}, u32[]{:S(2)}) collective-permute-start(bf16[2,128,1024]{1,2,0:T(8,128)(2,1)} %collective-permute-done), channel_id=1, source_target_pairs={{0,1},{1,2},{2,3},{3,4},{4,5},{5,6},{6,7},{7,8},{8,9},{9,10},{10,1... | collective-permute-start | bytes 1572872 | tf_op jit(solution)/shard_map/ppermute | solution.py:16
  53.1 3.5 %copy-start.56 = (f32[2,2,8,128]{3,2,1,0:T(8,128)}, f32[2,2,8,128]{3,2,1,0:T(8,128)S(1)}, u32[]{:S(2)}) copy-start(f32[2,2,8,128]{3,2,1,0:T(8,128)S(1)} %add_add_fusion.2) | copy-start | bytes 49156
  75.1 3.1 %copy-start.26 = (bf16[2,8,2,128,128]{3,4,2,1,0:T(8,128)(2,1)}, bf16[2,8,2,128,128]{3,4,2,1,0:T(8,128)(2,1)S(1)}, u32[]{:S(2)}) copy-start(bf16[2,8,2,128,128]{3,4,2,1,0:T(8,128)(2,1)S(1)} %fusion.5) | copy-start | bytes 3145732
  75.7 16.9 %collective-permute-start.5 = (f32[2,128,1024]{1,2,0:T(8,128)S(1)}, f32[2,128,1024]{1,2,0:T(8,128)S(1)}, u32[]{:S(2)}, u32[]{:S(2)}) collective-permute-start(f32[2,128,1024]{1,2,0:T(8,128)S(1)} %fusion.44), channel_id=1, source_target_pairs={{1,0},{2,1},{3,2},{4,3},{5,4},{6,5},{7,6},{8,7},{9,8},{10,9},{11,1... | collective-permute-start | bytes 3145736 | tf_op jit(solution)/shard_map/ppermute | solution.py:16
  79.8 12.9 %copy-start.6 = (f32[2,8,128,128,1]{3,2,4,1,0:T(8,128)}, f32[2,8,128,128,1]{3,2,4,1,0:T(8,128)S(1)}, u32[]{:S(2)}) copy-start(f32[2,8,128,128,1]{3,2,4,1,0:T(8,128)S(1)} %fusion.88) | copy-start | bytes 3145732
  80.8 13.3 %copy-start.27 = (f32[2,8,128,128,1]{2,3,4,1,0:T(8,128)}, f32[2,8,128,128,1]{2,3,4,1,0:T(8,128)S(1)}, u32[]{:S(2)}) copy-start(f32[2,8,128,128,1]{2,3,4,1,0:T(8,128)S(1)} %fusion.47) | copy-start | bytes 3145732
  94.1 17.3 %collective-permute-start.4 = (f32[2,128,1024]{1,2,0:T(8,128)}, f32[2,128,1024]{1,2,0:T(8,128)}, u32[]{:S(2)}, u32[]{:S(2)}) collective-permute-start(f32[2,128,1024]{1,2,0:T(8,128)} %get-tuple-element.45), channel_id=1, source_target_pairs={{0,1},{1,2},{2,3},{3,4},{4,5},{5,6},{6,7},{7,8},{8,9},{9,10},{10,1... | collective-permute-start | bytes 3145736 | tf_op jit(solution)/shard_map/ppermute | solution.py:16
  96.0 16.4 %collective-permute-start.6 = (f32[2,128,1024]{1,2,0:T(8,128)}, f32[2,128,1024]{1,2,0:T(8,128)}, u32[]{:S(2)}, u32[]{:S(2)}) collective-permute-start(f32[2,128,1024]{1,2,0:T(8,128)} %get-tuple-element.44), channel_id=1, source_target_pairs={{1,0},{2,1},{3,2},{4,3},{5,4},{6,5},{7,6},{8,7},{9,8},{10,9},{11,1... | collective-permute-start | bytes 3145736 | tf_op jit(solution)/shard_map/ppermute | solution.py:16
  111.3 4.2 %copy-start.25 = (f32[2,8,128,128,1]{2,3,4,1,0:T(8,128)}, f32[2,8,128,128,1]{2,3,4,1,0:T(8,128)S(1)}, u32[]{:S(2)}) copy-start(f32[2,8,128,128,1]{2,3,4,1,0:T(8,128)S(1)} %fusion.45) | copy-start | bytes 3145732
  112.4 5.1 %copy-start.15 = (f32[2,128,16,64]{3,2,1,0:T(8,128)S(1)}, f32[2,128,16,64]{3,2,1,0:T(8,128)}, u32[]{:S(2)}) copy-start(f32[2,128,16,64]{3,2,1,0:T(8,128)} %copy.325) | copy-start | bytes 3145732
  112.5 5.1 %copy-start.16 = (f32[2,128,16,64]{3,2,1,0:T(8,128)S(1)}, f32[2,128,16,64]{3,2,1,0:T(8,128)}, u32[]{:S(2)}) copy-start(f32[2,128,16,64]{3,2,1,0:T(8,128)} %copy.326) | copy-start | bytes 3145732
  115.5 18.2 %collective-permute-start.7 = (f32[2,128,1024]{1,2,0:T(8,128)}, f32[2,128,1024]{1,2,0:T(8,128)}, u32[]{:S(2)}, u32[]{:S(2)}) collective-permute-start(f32[2,128,1024]{1,2,0:T(8,128)} %get-tuple-element.43), channel_id=1, source_target_pairs={{0,1},{1,2},{2,3},{3,4},{4,5},{5,6},{6,7},{7,8},{8,9},{9,10},{10,1... | collective-permute-start | bytes 3145736 | tf_op jit(solution)/shard_map/ppermute | solution.py:16
  129.9 3.8 %copy-start.5 = (f32[2,8,128,128,1]{3,2,4,1,0:T(8,128)S(1)}, f32[2,8,128,128,1]{3,2,4,1,0:T(8,128)}, u32[]{:S(2)}) copy-start(f32[2,8,128,128,1]{3,2,4,1,0:T(8,128)} %copy-done.4) | copy-start | bytes 3145732
  (49 other events, 103.0 us)
where the time goes:
time: 236 us; the launch traced here: 235 us
  blocking collectives  91 us (39%)
  local copies, waits for them, and re-layouts  45.8 us (19%)
  other arithmetic  40.8 us (17%)
  starting transfers between devices  22.5 us (10%)
  matrix products  17.9 us (8%)
  waiting for transfers between devices  15.2 us (6%)
    psum x1, blocking collectives, shards(): lax.psum((grad_gain_q, grad_gain_k), ('dp', 'ctx'))  91 us
    unnamed x158, local copies, waits for them, and re-layouts  24.7 us
    ppermute x8, starting transfers between devices, from_behind(): return lax.ppermute(block, axis, route)  22.5 us
    ppermute x8, waiting for transfers between devices, from_behind(): return lax.ppermute(block, axis, route)  15.2 us
    reshape x2, local copies, waits for them, and re-layouts, shards(): cotangent_heads = cotangent.reshape(2, block, kv_heads, repeat, head_width)  6.23 us
    unnamed x1, other arithmetic  5.11 us
    convert_element_type x1, other arithmetic, shards(): grad_queries.reshape(2, block, -1).astype(jnp.bfloat16)  4.83 us
  transfers between devices with their start and end apart: 8, of which 3 were waited for; matrix products, arithmetic and copies ran while one was open for 23% of the time, Pallas kernels for 0%

commit v1 on v0

--- a/solution.py
+++ b/solution.py
@@ -194,7 +194,10 @@
     grad_v_flat = key_value_gradient[:, 1]
     grad_queries, grad_gain_q = q_back(grad_q_heads.reshape(2, block, q_heads, head_width))
     grad_keys, grad_gain_k = k_back(grad_k_heads)
-    grad_gain_q, grad_gain_k = lax.psum((grad_gain_q, grad_gain_k), ("dp", "ctx"))
+    store_turns = lambda v0, a_name, group_axis: lax.psum(
+        lax.psum(v0, axis_name=a_name), axis_name=group_axis
+    )
+    grad_gain_q, grad_gain_k = store_turns((grad_gain_q, grad_gain_k), "ctx", "dp")
     return (
         attended_heads.reshape(2, block, -1),
         grad_queries.reshape(2, block, -1).astype(jnp.bfloat16),

time: 236 us -> 294 us (1.25)
  the two profiles are of different devices: /device:TPU:1 before, /device:TPU:128 now
where the time goes in v1:
time: 294 us; the launch traced here: 293 us
  blocking collectives  138 us (47%)
  local copies, waits for them, and re-layouts  45.8 us (16%)
  other arithmetic  40.7 us (14%)
  starting transfers between devices  28.3 us (10%)
  waiting for transfers between devices  19.8 us (7%)
  matrix products  17.9 us (6%)
    psum x1, blocking collectives, shards(): lax.psum(v0, axis_name=a_name)  127 us
    ppermute x8, starting transfers between devices, from_behind(): return lax.ppermute(block, axis, route)  28.3 us
    unnamed x158, local copies, waits for them, and re-layouts  24.7 us
    ppermute x8, waiting for transfers between devices, from_behind(): return lax.ppermute(block, axis, route)  19.8 us
    psum x1, blocking collectives, shards(): lax.psum(lax.psum(v0, axis_name=a_name), axis_name=group_axis)  11 us
    reshape x2, local copies, waits for them, and re-layouts, shards(): cotangent_heads = cotangent.reshape(2, block, kv_heads, repeat, head_width)  6.24 us
  transfers between devices with their start and end apart: 8, of which 4 were waited for; matrix products, arithmetic and copies ran while one was open for 19% of the time, Pallas kernels for 0%

profile of v1, /device:TPU:128, one launch (start us, length us, event | category | flops | bytes accessed | tf_op | source)
XLA Modules:
  0.0 292.6 jit_solution(697410935277196893)
XLA Ops:
  8.4 3.9 %collective-permute-start.1 = (bf16[2,128,1024]{1,2,0:T(8,128)(2,1)}, bf16[2,128,1024]{1,2,0:T(8,128)(2,1)}, u32[]{:S(2)}, u32[]{:S(2)}) collective-permute-start(bf16[2,128,1024]{1,2,0:T(8,128)(2,1)} %fusion.65), channel_id=1, source_target_pairs={{1,0},{2,1},{3,2},{4,3},{5,4},{6,5},{7,6},{8,7},{9,8},{10,9},{11,1... | collective-permute-start | bytes 1572872 | tf_op jit(solution)/shard_map/ppermute | solution.py:16
  16.1 2.0 copy.219
  18.0 2.0 copy.220
  20.2 2.9 fusion.3
  24.2 2.1 broadcast_select_fusion
  26.2 1.9 collective-permute-start
  28.2 2.4 fusion.15
  30.6 7.0 %collective-permute-start.3 = (bf16[2,128,1024]{1,2,0:T(8,128)(2,1)}, bf16[2,128,1024]{1,2,0:T(8,128)(2,1)}, u32[]{:S(2)}, u32[]{:S(2)}) collective-permute-start(bf16[2,128,1024]{1,2,0:T(8,128)(2,1)} %get-tuple-element.50), channel_id=1, source_target_pairs={{1,0},{2,1},{3,2},{4,3},{5,4},{6,5},{7,6},{8,7},{9,8},{10,9},{11,1... | collective-permute-start | bytes 1572872 | tf_op jit(solution)/shard_map/ppermute | solution.py:16
  38.4 2.6 reshape.655
  40.9 3.7 %copy.247 = bf16[2,128,8,2,128]{1,4,3,2,0:T(8,128)(2,1)} copy(bf16[2,128,8,2,128]{4,3,2,1,0:T(2,128)(2,1)} %reshape.655) | data formatting | bytes 2097152 | tf_op jit(solution)/shard_map/reshape | solution.py:132
  44.6 2.2 collective-permute-start.2
  50.8 8.0 %collective-permute-done.2 = bf16[2,128,1024]{1,2,0:T(8,128)(2,1)S(1)} collective-permute-done((bf16[2,128,1024]{1,2,0:T(8,128)(2,1)}, bf16[2,128,1024]{1,2,0:T(8,128)(2,1)S(1)}, u32[]{:S(2)}, u32[]{:S(2)}) %collective-permute-start.2) | collective-permute-done | bytes 524320 | tf_op jit(solution)/shard_map/ppermute | solution.py:16
  62.0 2.4 bitcast_convert_fusion
  64.3 4.2 %copy.285 = f32[2,8,2,128,128]{4,2,1,3,0:T(2,128)} copy(f32[2,8,2,128,128]{3,4,2,1,0:T(8,128)} %get-tuple-element.92) | data formatting | bytes 4194304
  68.5 5.1 %multiply_reduce_fusion = f32[2,8,2,128]{2,1,3,0:T(8,128)} fusion(f32[2,8,2,128,128]{4,2,1,3,0:T(2,128)} %copy.285, bf16[2,128,8,2,128]{4,3,2,1,0:T(2,128)(2,1)} %reshape.655), kind=kLoop, calls=%fused_computation.40 | loop fusion | flops 1568768 | bytes 3162112
  73.6 2.2 copy.286
  75.8 2.5 fusion.49
  83.5 2.1 collective-permute-start.5
  88.5 9.3 %collective-permute-done.5 = f32[2,128,1024]{1,2,0:T(8,128)S(1)} collective-permute-done((f32[2,128,1024]{1,2,0:T(8,128)S(1)}, f32[2,128,1024]{1,2,0:T(8,128)S(1)}, u32[]{:S(2)}, u32[]{:S(2)}) %collective-permute-start.5) | collective-permute-done | bytes 1048608 | tf_op jit(solution)/shard_map/ppermute | solution.py:16
  99.3 1.9 collective-permute-start.4
  101.2 7.4 %collective-permute-start.6 = (f32[2,128,1024]{1,2,0:T(8,128)}, f32[2,128,1024]{1,2,0:T(8,128)}, u32[]{:S(2)}, u32[]{:S(2)}) collective-permute-start(f32[2,128,1024]{1,2,0:T(8,128)} %get-tuple-element.46), channel_id=1, source_target_pairs={{1,0},{2,1},{3,2},{4,3},{5,4},{6,5},{7,6},{8,7},{9,8},{10,9},{11,1... | collective-permute-start | bytes 3145736 | tf_op jit(solution)/shard_map/ppermute | solution.py:16
  110.1 3.3 %copy.325 = f32[2,128,16,64]{3,2,1,0:T(8,128)} copy(f32[2,128,16,64]{1,3,2,0:T(8,128)} %get-tuple-element.60) | data formatting | bytes 2097152
  113.4 3.3 %copy.326 = f32[2,128,16,64]{3,2,1,0:T(8,128)} copy(f32[2,128,16,64]{1,3,2,0:T(8,128)} %get-tuple-element.61) | data formatting | bytes 2097152
  116.7 1.9 fusion.89
  121.0 3.0 %fusion.32 = (f32[1,2,128,1024]{2,3,1,0:T(8,128)S(1)}, f32[2,128,1024]{1,2,0:T(8,128)}) fusion(f32[2,1,128,1024]{2,3,1,0:T(8,128)S(1)} %bitcast.301, f32[2,1,128,1024]{2,3,1,0:T(8,128)S(1)} %bitcast.319, f32[2,128,1024]{1,2,0:T(8,128)} %collective-permute-done.6, pred[]{:T(512)S(6)} %eq.6, f32[2,1,128,1024]{2,3,1,0:T(8,128)S(1)} %bitcast.323, ...), kind=kLoop, calls=%fused_computation.63 | loop fusion | flops 1572864 | bytes 8388610 | tf_op jit(solution)/shard_map/stack | solution.py:192
  124.0 2.0 collective-permute-start.7
  126.7 2.5 multiply_reduce_fusion.1
  133.6 4.8 %fusion = bf16[2,128,16,128]{3,2,1,0:T(8,128)(2,1)} fusion(f32[2,128,16]{2,1,0:T(8,128)} %copy.243, f32[128]{0:T(128)} %param.11, f32[2,128,16]{2,1,0:T(8,128)S(1)} %copy.218, f32[2,128,16,64]{3,2,1,0:T(8,128)} %copy-done.1, f32[2,128,16,64]{3,2,1,0:T(8,128)} %copy-done, f32[2,128,16,128]{3,2,1,0:T(8,128)S(1)} %bitcast.300), kind=kLoop, calls=%fused_computation.1 | loop fusion | flops 3670016 | bytes 5276160 | tf_op jit(solution)/shard_map/convert_element_type | solution.py:203
  138.5 2.4 convert_element_type.84
  142.2 1.9 collective-permute-done.7
  154.3 127.4 %all-reduce.4 = (f32[128]{0:T(128)S(1)}, f32[128]{0:T(128)S(1)}) all-reduce(f32[128]{0:T(128)S(1)} %copy-done.72, f32[128]{0:T(128)S(1)} %get-tuple-element.38), channel_id=1, replica_groups=mesh['dp'=4,'ctx'=64] {'ctx'}, use_global_device_ids=true, to_apply=%region_8.9 | all-reduce | flops 256 | bytes 2048 | tf_op jit(solution)/shard_map/psum | solution.py:198
  281.6 11.0 %all-reduce.5 = (f32[128]{0:T(128)}, f32[128]{0:T(128)}) all-reduce(f32[128]{0:T(128)S(1)} %get-tuple-element.40, f32[128]{0:T(128)S(1)} %get-tuple-element.41), channel_id=1, replica_groups=mesh['dp'=4,'ctx'=64] {'dp'}, use_global_device_ids=true, to_apply=%region_9.10 | all-reduce | flops 256 | bytes 2048 | tf_op jit(solution)/shard_map/psum | solution.py:197
  (217 shorter events, 49.8 us)
Async XLA Ops:
  0.6 4.7 %copy-start.61 = (f32[128]{0:T(128)S(1)}, f32[128]{0:T(128)}, u32[]{:S(2)}) copy-start(f32[128]{0:T(128)} %param.12) | copy-start | bytes 1540
  6.5 5.8 %copy-start.8 = (bf16[2,128,8,128]{3,1,2,0:T(8,128)(2,1)}, bf16[2,128,8,128]{3,1,2,0:T(8,128)(2,1)S(1)}, u32[]{:S(2)}) copy-start(bf16[2,128,8,128]{3,1,2,0:T(8,128)(2,1)S(1)} %maximum_convert_fusion) | copy-start | bytes 1572868
  7.2 5.1 %copy-start.19 = (bf16[2,128,8,128]{1,3,2,0:T(8,128)(2,1)}, bf16[2,128,8,128]{1,3,2,0:T(8,128)(2,1)S(1)}, u32[]{:S(2)}) copy-start(bf16[2,128,8,128]{1,3,2,0:T(8,128)(2,1)S(1)} %copy.223) | copy-start | bytes 1572868
  7.5 4.8 %copy-start.21 = (bf16[2,128,1024]{1,2,0:T(8,128)(2,1)}, bf16[2,128,1024]{1,2,0:T(8,128)(2,1)S(1)}, u32[]{:S(2)}) copy-start(bf16[2,128,1024]{1,2,0:T(8,128)(2,1)S(1)} %copy.224) | copy-start | bytes 1572868
  8.4 15.8 %collective-permute-start.1 = (bf16[2,128,1024]{1,2,0:T(8,128)(2,1)}, bf16[2,128,1024]{1,2,0:T(8,128)(2,1)}, u32[]{:S(2)}, u32[]{:S(2)}) collective-permute-start(bf16[2,128,1024]{1,2,0:T(8,128)(2,1)} %fusion.65), channel_id=1, source_target_pairs={{1,0},{2,1},{3,2},{4,3},{5,4},{6,5},{7,6},{8,7},{9,8},{10,9},{11,1... | collective-permute-start | bytes 1572872 | tf_op jit(solution)/shard_map/ppermute | solution.py:16
  20.1 3.1 %copy-start.63 = (pred[2]{0:T(512)(128)(4,1)S(1)}, pred[2]{0:T(512)(128)(4,1)}, u32[]{:S(2)}) copy-start(pred[2]{0:T(512)(128)(4,1)} %get-tuple-element.80) | copy-start | bytes 10
  20.1 3.1 %copy-start.64 = (pred[2]{0:T(512)(128)(4,1)S(1)}, pred[2]{0:T(512)(128)(4,1)}, u32[]{:S(2)}) copy-start(pred[2]{0:T(512)(128)(4,1)} %get-tuple-element.81) | copy-start | bytes 10
  20.1 3.1 %copy-start.65 = (pred[2]{0:T(512)(128)(4,1)S(1)}, pred[2]{0:T(512)(128)(4,1)}, u32[]{:S(2)}) copy-start(pred[2]{0:T(512)(128)(4,1)} %get-tuple-element.82) | copy-start | bytes 10
  20.1 3.1 %copy-start.66 = (pred[2]{0:T(512)(128)(4,1)S(1)}, pred[2]{0:T(512)(128)(4,1)}, u32[]{:S(2)}) copy-start(pred[2]{0:T(512)(128)(4,1)} %get-tuple-element.83) | copy-start | bytes 10
  20.2 3.1 %copy-start.58 = (s32[2,128]{1,0:T(2,128)S(1)}, s32[2,128]{1,0:T(2,128)}, u32[]{:S(2)}) copy-start(s32[2,128]{1,0:T(2,128)} %get-tuple-element.53) | copy-start | bytes 3076
  20.2 3.1 %copy-start.71 = (s32[2,128]{1,0:T(2,128)S(1)}, s32[2,128]{1,0:T(2,128)}, u32[]{:S(2)}) copy-start(s32[2,128]{1,0:T(2,128)} %param.10) | copy-start | bytes 3076
  20.2 3.9 %copy-start.20 = (bf16[2,128,8,128]{1,3,2,0:T(8,128)(2,1)S(1)}, bf16[2,128,8,128]{1,3,2,0:T(8,128)(2,1)}, u32[]{:S(2)}) copy-start(bf16[2,128,8,128]{1,3,2,0:T(8,128)(2,1)} %copy-done.19) | copy-start | bytes 1572868
  20.2 3.9 %copy-start.22 = (bf16[2,128,1024]{1,2,0:T(8,128)(2,1)S(1)}, bf16[2,128,1024]{1,2,0:T(8,128)(2,1)}, u32[]{:S(2)}) copy-start(bf16[2,128,1024]{1,2,0:T(8,128)(2,1)} %copy-done.21) | copy-start | bytes 1572868
  23.2 5.0 %copy-start.9 = (bf16[2,128,8,128]{3,1,2,0:T(8,128)(2,1)S(1)}, bf16[2,128,8,128]{3,1,2,0:T(8,128)(2,1)}, u32[]{:S(2)}) copy-start(bf16[2,128,8,128]{3,1,2,0:T(8,128)(2,1)} %copy-done.8) | copy-start | bytes 1572868
  24.1 6.5 %copy-start.49 = (pred[2,128,128]{1,2,0:T(8,128)(4,1)}, pred[2,128,128]{1,2,0:T(8,128)(4,1)S(1)}, u32[]{:S(2)}) copy-start(pred[2,128,128]{1,2,0:T(8,128)(4,1)S(1)} %get-tuple-element.70) | copy-start | bytes 98308
  26.2 18.4 %collective-permute-start = (bf16[2,128,1024]{1,2,0:T(8,128)(2,1)}, bf16[2,128,1024]{1,2,0:T(8,128)(2,1)}, u32[]{:S(2)}, u32[]{:S(2)}) collective-permute-start(bf16[2,128,1024]{1,2,0:T(8,128)(2,1)} %get-tuple-element.51), channel_id=1, source_target_pairs={{0,1},{1,2},{2,3},{3,4},{4,5},{5,6},{6,7},{7,8},{8,9},{9,10},{10,1... | collective-permute-start | bytes 1572872 | tf_op jit(solution)/shard_map/ppermute | solution.py:16
  30.6 18.2 %collective-permute-start.3 = (bf16[2,128,1024]{1,2,0:T(8,128)(2,1)}, bf16[2,128,1024]{1,2,0:T(8,128)(2,1)}, u32[]{:S(2)}, u32[]{:S(2)}) collective-permute-start(bf16[2,128,1024]{1,2,0:T(8,128)(2,1)} %get-tuple-element.50), channel_id=1, source_target_pairs={{1,0},{2,1},{3,2},{4,3},{5,4},{6,5},{7,6},{8,7},{9,8},{10,9},{11,1... | collective-permute-start | bytes 1572872 | tf_op jit(solution)/shard_map/ppermute | solution.py:16
  44.6 3.5 %copy-start.43 = (pred[2,128,128]{1,2,0:T(8,128)(4,1)S(1)}, pred[2,128,128]{1,2,0:T(8,128)(4,1)}, u32[]{:S(2)}) copy-start(pred[2,128,128]{1,2,0:T(8,128)(4,1)} %get-tuple-element.72) | copy-start | bytes 98308
  44.6 14.2 %collective-permute-start.2 = (bf16[2,128,1024]{1,2,0:T(8,128)(2,1)}, bf16[2,128,1024]{1,2,0:T(8,128)(2,1)S(1)}, u32[]{:S(2)}, u32[]{:S(2)}) collective-permute-start(bf16[2,128,1024]{1,2,0:T(8,128)(2,1)} %collective-permute-done), channel_id=1, source_target_pairs={{0,1},{1,2},{2,3},{3,4},{4,5},{5,6},{6,7},{7,8},{8,9},{9,10},{10,1... | collective-permute-start | bytes 1572872 | tf_op jit(solution)/shard_map/ppermute | solution.py:16
  50.8 8.1 %copy-start.45 = (pred[2,128,128]{1,2,0:T(8,128)(4,1)S(1)}, pred[2,128,128]{1,2,0:T(8,128)(4,1)}, u32[]{:S(2)}) copy-start(pred[2,128,128]{1,2,0:T(8,128)(4,1)} %get-tuple-element.71) | copy-start | bytes 98308
  60.9 3.5 %copy-start.56 = (f32[2,2,8,128]{3,2,1,0:T(8,128)}, f32[2,2,8,128]{3,2,1,0:T(8,128)S(1)}, u32[]{:S(2)}) copy-start(f32[2,2,8,128]{3,2,1,0:T(8,128)S(1)} %add_add_fusion.2) | copy-start | bytes 49156
  82.9 3.1 %copy-start.26 = (bf16[2,8,2,128,128]{3,4,2,1,0:T(8,128)(2,1)}, bf16[2,8,2,128,128]{3,4,2,1,0:T(8,128)(2,1)S(1)}, u32[]{:S(2)}) copy-start(bf16[2,8,2,128,128]{3,4,2,1,0:T(8,128)(2,1)S(1)} %fusion.5) | copy-start | bytes 3145732
  83.5 14.4 %collective-permute-start.5 = (f32[2,128,1024]{1,2,0:T(8,128)S(1)}, f32[2,128,1024]{1,2,0:T(8,128)S(1)}, u32[]{:S(2)}, u32[]{:S(2)}) collective-permute-start(f32[2,128,1024]{1,2,0:T(8,128)S(1)} %fusion.44), channel_id=1, source_target_pairs={{1,0},{2,1},{3,2},{4,3},{5,4},{6,5},{7,6},{8,7},{9,8},{10,9},{11,1... | collective-permute-start | bytes 3145736 | tf_op jit(solution)/shard_map/ppermute | solution.py:16
  87.5 10.3 %copy-start.6 = (f32[2,8,128,128,1]{3,2,4,1,0:T(8,128)}, f32[2,8,128,128,1]{3,2,4,1,0:T(8,128)S(1)}, u32[]{:S(2)}) copy-start(f32[2,8,128,128,1]{3,2,4,1,0:T(8,128)S(1)} %fusion.88) | copy-start | bytes 3145732
  88.5 10.8 %copy-start.27 = (f32[2,8,128,128,1]{2,3,4,1,0:T(8,128)}, f32[2,8,128,128,1]{2,3,4,1,0:T(8,128)S(1)}, u32[]{:S(2)}) copy-start(f32[2,8,128,128,1]{2,3,4,1,0:T(8,128)S(1)} %fusion.47) | copy-start | bytes 3145732
  99.3 21.1 %collective-permute-start.4 = (f32[2,128,1024]{1,2,0:T(8,128)}, f32[2,128,1024]{1,2,0:T(8,128)}, u32[]{:S(2)}, u32[]{:S(2)}) collective-permute-start(f32[2,128,1024]{1,2,0:T(8,128)} %get-tuple-element.47), channel_id=1, source_target_pairs={{0,1},{1,2},{2,3},{3,4},{4,5},{5,6},{6,7},{7,8},{8,9},{9,10},{10,1... | collective-permute-start | bytes 3145736 | tf_op jit(solution)/shard_map/ppermute | solution.py:16
  101.2 19.8 %collective-permute-start.6 = (f32[2,128,1024]{1,2,0:T(8,128)}, f32[2,128,1024]{1,2,0:T(8,128)}, u32[]{:S(2)}, u32[]{:S(2)}) collective-permute-start(f32[2,128,1024]{1,2,0:T(8,128)} %get-tuple-element.46), channel_id=1, source_target_pairs={{1,0},{2,1},{3,2},{4,3},{5,4},{6,5},{7,6},{8,7},{9,8},{10,9},{11,1... | collective-permute-start | bytes 3145736 | tf_op jit(solution)/shard_map/ppermute | solution.py:16
  120.3 3.7 %copy-start.25 = (f32[2,8,128,128,1]{2,3,4,1,0:T(8,128)}, f32[2,8,128,128,1]{2,3,4,1,0:T(8,128)S(1)}, u32[]{:S(2)}) copy-start(f32[2,8,128,128,1]{2,3,4,1,0:T(8,128)S(1)} %fusion.45) | copy-start | bytes 3145732
  121.0 5.1 %copy-start.15 = (f32[2,128,16,64]{3,2,1,0:T(8,128)S(1)}, f32[2,128,16,64]{3,2,1,0:T(8,128)}, u32[]{:S(2)}) copy-start(f32[2,128,16,64]{3,2,1,0:T(8,128)} %copy.325) | copy-start | bytes 3145732
  121.0 5.1 %copy-start.16 = (f32[2,128,16,64]{3,2,1,0:T(8,128)S(1)}, f32[2,128,16,64]{3,2,1,0:T(8,128)}, u32[]{:S(2)}) copy-start(f32[2,128,16,64]{3,2,1,0:T(8,128)} %copy.326) | copy-start | bytes 3145732
  124.0 20.1 %collective-permute-start.7 = (f32[2,128,1024]{1,2,0:T(8,128)}, f32[2,128,1024]{1,2,0:T(8,128)}, u32[]{:S(2)}, u32[]{:S(2)}) collective-permute-start(f32[2,128,1024]{1,2,0:T(8,128)} %get-tuple-element.45), channel_id=1, source_target_pairs={{0,1},{1,2},{2,3},{3,4},{4,5},{5,6},{6,7},{7,8},{8,9},{9,10},{10,1... | collective-permute-start | bytes 3145736 | tf_op jit(solution)/shard_map/ppermute | solution.py:16
  138.5 5.6 %copy-start.5 = (f32[2,8,128,128,1]{3,2,4,1,0:T(8,128)S(1)}, f32[2,8,128,128,1]{3,2,4,1,0:T(8,128)}, u32[]{:S(2)}) copy-start(f32[2,8,128,128,1]{3,2,4,1,0:T(8,128)} %copy-done.4) | copy-start | bytes 3145732
  (49 other events, 102.3 us)
